TPU v7x, 256 devices: a whole 4x4x8 slice. The times are simulated.
256 devices in a mesh: row: 16 (over x_lo, y, core), col: 16 (over x_hi, z).
Axes of the slice: x: 4 (x_hi: 2, x_lo: 2; x = x_hi * 2 + x_lo), y: 4, z: 8, core: 2. Of those that a mesh axis runs over, the one named last changes fastest.
Arguments:
- node_features: bfloat16 [65536, 256], P(('row', 'col')), may hold values from -6 to 6
- tile_values: bfloat16 [16, 16, 128, 128, 128], P('row', 'col'), may hold values from -0.09375 to 0.09375
- tile_coords: int32 [16, 16, 128, 2], P('row', 'col'), may hold values from 0 to 31, as said below
- tile_counts: int32 [16, 16], P('row', 'col'), may hold values from 32 to 128, as said below
- first_weight: bfloat16 [256, 256], replicated, may hold values from -0.375 to 0.375
- second_weight: bfloat16 [256, 128], replicated, may hold values from -0.375 to 0.375
- out_grad: bfloat16 [65536, 128], P(('row', 'col')), may hold values from -6 to 6
Outputs:
- output: bfloat16 [65536, 128], P(('row', 'col'))
- first_grad: float32 [256, 256], replicated
- second_grad: float32 [256, 128], replicated
Inputs may be any that keep to these rules, and one draw needn't show every extreme that they name: `tile_counts`: each grid cell uses at least 32 slots; at least one grid cell uses all 128 in every draw. `tile_coords`: the first entry is a tile row below 32, the second a tile column below 32; within one grid cell no two slots share a position.
All inputs are finite; a program needn't handle non-finite values.
Results may differ from a plain program's by a relative error of at most 0.005.
Values may be sent and summed in bfloat16 or wider, within the bound.
A program may use at most 64 MiB of HBM per device.

v0:
```python
import math
import jax
import jax.numpy as jnp
from jax import lax
from jax.sharding import PartitionSpec as P

HIGHEST = lax.Precision.HIGHEST


def tile_sum(tile_block, dest_index, source_index, live_slots, source, dest_tiles, flipped):
    slot_count = tile_block.shape[0]
    group_size = math.gcd(slot_count, 32)
    round_count = slot_count // group_size
    edge_size = tile_block.shape[1]
    width_size = source.shape[-1]
    grouped_tiles = tile_block.reshape(round_count, group_size, edge_size, edge_size)
    grouped_dest = dest_index.reshape(round_count, group_size)
    grouped_source = source_index.reshape(round_count, group_size)
    grouped_live = live_slots.reshape(round_count, group_size)
    target_ids = jnp.arange(dest_tiles, dtype=jnp.int32)
    einsum_form = "tba,tbw->taw" if flipped else "tab,tbw->taw"

    def add_group(running, pieces):
        group_tiles, group_dest, group_source, group_live = pieces
        picked = jnp.take(source, group_source, axis=0)
        products = jnp.einsum(einsum_form, group_tiles, picked, preferred_element_type=jnp.float32)
        select = ((group_dest[:, None] == target_ids[None, :]) & group_live[:, None]).astype(
            jnp.float32
        )
        running = running + jnp.einsum("tr,taw->raw", select, products, precision=HIGHEST)
        return (running, None)

    start_sum = jnp.zeros((dest_tiles, edge_size, width_size), jnp.float32)
    running, unused = lax.scan(
        add_group, start_sum, (grouped_tiles, grouped_dest, grouped_source, grouped_live)
    )
    return running.reshape(dest_tiles * edge_size, width_size)


def on_device(
    node_features, tile_values, tile_coords, tile_counts, first_weight, second_weight, out_grad
):
    node_rows = node_features.shape[0]
    edge_size = tile_values.shape[-1]
    slot_count = tile_values.shape[2]
    grid_rows = lax.axis_size("row")
    grid_cols = lax.axis_size("col")
    row_tiles = grid_rows * node_rows // edge_size
    col_tiles = grid_cols * node_rows // edge_size
    tile_block = tile_values.reshape(slot_count, edge_size, edge_size)
    flat_coords = tile_coords.reshape(slot_count, 2)
    tile_row = flat_coords[:, 0]
    tile_col = flat_coords[:, 1]
    live_slots = jnp.arange(slot_count, dtype=jnp.int32) < tile_counts.reshape(())
    gathered_x = lax.all_gather(node_features, "col", axis=0, tiled=True)
    feature_part = tile_sum(
        tile_block,
        tile_row,
        tile_col,
        live_slots,
        gathered_x.reshape(col_tiles, edge_size, -1),
        row_tiles,
        False,
    )
    first_mean = lax.psum_scatter(feature_part, "row", scatter_dimension=0, tiled=True)
    first_pre = jnp.dot(first_mean, first_weight.astype(jnp.float32), precision=HIGHEST)
    hidden_act = jax.nn.silu(first_pre).astype(jnp.bfloat16)
    second_wide = second_weight.astype(jnp.float32)
    gathered_h = lax.all_gather(hidden_act, "col", axis=0, tiled=True)
    hidden_part = tile_sum(
        tile_block,
        tile_row,
        tile_col,
        live_slots,
        gathered_h.reshape(col_tiles, edge_size, -1),
        row_tiles,
        False,
    )
    second_mean = lax.psum_scatter(hidden_part, "row", scatter_dimension=0, tiled=True)
    logit_rows = jnp.dot(second_mean, second_wide, precision=HIGHEST)
    output = logit_rows.astype(jnp.bfloat16)
    gathered_g = lax.all_gather(out_grad, "row", axis=0, tiled=True)
    grad_part = tile_sum(
        tile_block,
        tile_col,
        tile_row,
        live_slots,
        gathered_g.reshape(row_tiles, edge_size, -1),
        col_tiles,
        True,
    )
    back_sum = lax.psum_scatter(grad_part, "col", scatter_dimension=0, tiled=True)
    scale = 1.0 / math.sqrt(node_rows * grid_rows * grid_cols)
    second_local = jnp.dot(hidden_act.astype(jnp.float32).T, back_sum, precision=HIGHEST) * scale
    hidden_grad = jnp.dot(back_sum, second_wide.T, precision=HIGHEST)
    sigma = jax.nn.sigmoid(first_pre)
    pre_grad = hidden_grad * (sigma * (1.0 + first_pre * (1.0 - sigma)))
    second_grad = lax.psum(second_local, ("row", "col"))
    first_local = jnp.dot(first_mean.T, pre_grad, precision=HIGHEST) * scale
    first_grad = lax.psum(first_local, ("row", "col"))
    return (output, first_grad, second_grad)


def solution(mesh):
    return jax.shard_map(
        on_device,
        mesh=mesh,
        in_specs=(
            P(("row", "col"), None),
            P("row", "col", None, None, None),
            P("row", "col", None, None),
            P("row", "col"),
            P(),
            P(),
            P(("row", "col"), None),
        ),
        out_specs=(P(("row", "col"), None), P(), P()),
        check_vma=False,
    )
```

profile of v0, /device:TPU:1, one launch (start us, length us, event | category | flops | bytes accessed | tf_op | source)
XLA Modules:
  0.0 898.8 jit_solution(9143985936863349914)
XLA Ops:
  9.6 86.8 %all-gather.4.cloned.1.call-done = bf16[4096,256]{1,0:T(8,128)(2,1)} async-done(((bf16[256,256]{1,0:T(8,128)(2,1)}), bf16[4096,256]{1,0:T(8,128)(2,1)}) %all-gather.4.cloned.1.call-update) | async-done | bytes 2097168 | tf_op jit(solution)/shard_map/all_gather | solution.py:55
  96.3 64.7 %while.33 = (s32[]{:T(128)}, f32[32,128,256]{2,0,1:T(8,128)}, s32[4,32]{1,0:T(4,128)S(1)}, pred[4,32]{1,0:T(4,128)(4,1)S(1)}, bf16[4,32,128,128]{3,2,1,0:T(8,128...) while((s32[]{:T(128)}, f32[32,128,256]{2,0,1:T(8,128)}, ...), condition=%wide.region_1.3_spmd.clone, body=%wide.region_0.2_spmd.clone.sunk | while | flops 674237632 | bytes 24123028 | solution.py:34
  102.6 8.9 select_add_fusion.6
  117.9 10.2 %select_add_fusion.6 = f32[32,128,256]{2,0,1:T(8,128)} fusion(f32[32,128,256]{2,0,1:T(8,128)} %get-tuple-element.410, f32[32,128,256]{2,1,0:T(8,128)} %fusion.96, pred[]{:T(512)S(6)} %compare.9, s32[32]{0:T(128)S(1)} %fusion.97, pred[32]{0:T(512)(128)(4,1)S(1)} %dynamic-slice_bitcast_fusion.6), kind=kOutput, calls=%fused_computation.33.clone.1 | convolution fusion | flops 404752384 | bytes 12583073 | tf_op jit(solution)/shard_map/while/body/eval_jaxpr/tr,taw->raw/dot_general | solution.py:30
  134.4 10.2 %select_add_fusion.6 = f32[32,128,256]{2,0,1:T(8,128)} fusion(f32[32,128,256]{2,0,1:T(8,128)} %get-tuple-element.410, f32[32,128,256]{2,1,0:T(8,128)} %fusion.96, pred[]{:T(512)S(6)} %compare.9, s32[32]{0:T(128)S(1)} %fusion.97, pred[32]{0:T(512)(128)(4,1)S(1)} %dynamic-slice_bitcast_fusion.6), kind=kOutput, calls=%fused_computation.33.clone.1 | convolution fusion | flops 404752384 | bytes 12583073 | tf_op jit(solution)/shard_map/while/body/eval_jaxpr/tr,taw->raw/dot_general | solution.py:30
  150.9 10.2 %select_add_fusion.6 = f32[32,128,256]{2,0,1:T(8,128)} fusion(f32[32,128,256]{2,0,1:T(8,128)} %get-tuple-element.410, f32[32,128,256]{2,1,0:T(8,128)} %fusion.96, pred[]{:T(512)S(6)} %compare.9, s32[32]{0:T(128)S(1)} %fusion.97, pred[32]{0:T(512)(128)(4,1)S(1)} %dynamic-slice_bitcast_fusion.6), kind=kOutput, calls=%fused_computation.33.clone.1 | convolution fusion | flops 404752384 | bytes 12583073 | tf_op jit(solution)/shard_map/while/body/eval_jaxpr/tr,taw->raw/dot_general | solution.py:30
  161.0 6.6 copy.10
  168.5 65.5 %reduce-scatter.4.cloned.1.call-done = f32[256,256]{1,0:T(8,128)} async-done(((f32[4096,256]{1,0:T(8,128)}), f32[256,256]{1,0:T(8,128)}) %reduce-scatter.4.cloned.1.call-update) | async-done | bytes 262160 | tf_op jit(solution)/shard_map/reduce_scatter | solution.py:65
  236.2 37.0 %all-gather.8.cloned.1.call-done = bf16[4096,128]{1,0:T(8,128)(2,1)} async-done(((bf16[256,128]{1,0:T(8,128)(2,1)}), bf16[4096,128]{1,0:T(8,128)(2,1)}) %all-gather.8.cloned.1.call-update) | async-done | bytes 1048592 | tf_op jit(solution)/shard_map/all_gather | solution.py:82
  273.2 35.7 %while.35 = (s32[]{:T(128)}, f32[32,128,128]{2,0,1:T(8,128)}, s32[4,32]{1,0:T(4,128)S(1)}, pred[4,32]{1,0:T(4,128)(4,1)S(1)}, bf16[4,32,128,128]{3,2,1,0:T(8,128...) while((s32[]{:T(128)}, f32[32,128,128]{2,0,1:T(8,128)}, ...), condition=%wide.region_7.9_spmd.clone, body=%wide.region_6.8_spmd.clone.sunk | while | flops 337120544 | bytes 12588823 | solution.py:34
  284.7 5.4 select_add_fusion.8
  294.0 5.5 select_add_fusion.8
  303.4 5.5 select_add_fusion.8
  308.8 4.2 copy.12
  313.0 44.8 %all-gather.6.cloned.1.call-done = bf16[4096,256]{1,0:T(8,128)(2,1)} async-done(((bf16[256,256]{1,0:T(8,128)(2,1)}), bf16[4096,256]{1,0:T(8,128)(2,1)}) %all-gather.6.cloned.1.call-update) | async-done | bytes 2097168 | tf_op jit(solution)/shard_map/all_gather | solution.py:69
  357.8 65.0 %while.34 = (s32[]{:T(128)}, f32[32,128,256]{2,0,1:T(8,128)}, s32[4,32]{1,0:T(4,128)S(1)}, pred[4,32]{1,0:T(4,128)(4,1)S(1)}, bf16[4,32,128,128]{3,2,1,0:T(8,128...) while((s32[]{:T(128)}, f32[32,128,256]{2,0,1:T(8,128)}, ...), condition=%wide.region_4.6_spmd.clone, body=%wide.region_3.5_spmd.clone.sunk | while | flops 674237632 | bytes 24123028 | solution.py:34
  364.1 8.9 select_add_fusion.7
  379.4 10.2 %select_add_fusion.7 = f32[32,128,256]{2,0,1:T(8,128)} fusion(f32[32,128,256]{2,0,1:T(8,128)} %get-tuple-element.437, f32[32,128,256]{2,1,0:T(8,128)} %fusion.102, pred[]{:T(512)S(6)} %compare.10, s32[32]{0:T(128)S(1)} %fusion.103, pred[32]{0:T(512)(128)(4,1)S(1)} %dynamic-slice_bitcast_fusion.7), kind=kOutput, calls=%fused_computation.57.clone.1 | convolution fusion | flops 404752384 | bytes 12583073 | tf_op jit(solution)/shard_map/while/body/eval_jaxpr/tr,taw->raw/dot_general | solution.py:30
  396.0 10.3 %select_add_fusion.7 = f32[32,128,256]{2,0,1:T(8,128)} fusion(f32[32,128,256]{2,0,1:T(8,128)} %get-tuple-element.437, f32[32,128,256]{2,1,0:T(8,128)} %fusion.102, pred[]{:T(512)S(6)} %compare.10, s32[32]{0:T(128)S(1)} %fusion.103, pred[32]{0:T(512)(128)(4,1)S(1)} %dynamic-slice_bitcast_fusion.7), kind=kOutput, calls=%fused_computation.57.clone.1 | convolution fusion | flops 404752384 | bytes 12583073 | tf_op jit(solution)/shard_map/while/body/eval_jaxpr/tr,taw->raw/dot_general | solution.py:30
  412.6 10.2 %select_add_fusion.7 = f32[32,128,256]{2,0,1:T(8,128)} fusion(f32[32,128,256]{2,0,1:T(8,128)} %get-tuple-element.437, f32[32,128,256]{2,1,0:T(8,128)} %fusion.102, pred[]{:T(512)S(6)} %compare.10, s32[32]{0:T(128)S(1)} %fusion.103, pred[32]{0:T(512)(128)(4,1)S(1)} %dynamic-slice_bitcast_fusion.7), kind=kOutput, calls=%fused_computation.57.clone.1 | convolution fusion | flops 404752384 | bytes 12583073 | tf_op jit(solution)/shard_map/while/body/eval_jaxpr/tr,taw->raw/dot_general | solution.py:30
  422.8 6.6 copy.11
  429.5 131.3 %reduce-scatter.8.cloned.1.call-done = f32[256,128]{1,0:T(8,128)} async-done(((f32[4096,128]{1,0:T(8,128)}), f32[256,128]{1,0:T(8,128)}) %reduce-scatter.8.cloned.1.call-update) | async-done | bytes 131088 | tf_op jit(solution)/shard_map/reduce_scatter | solution.py:92
  565.2 67.1 %reduce-scatter.6.cloned.1.call-done = f32[256,256]{1,0:T(8,128)} async-done(((f32[4096,256]{1,0:T(8,128)}), f32[256,256]{1,0:T(8,128)}) %reduce-scatter.6.cloned.1.call-update) | async-done | bytes 262160 | tf_op jit(solution)/shard_map/reduce_scatter | solution.py:79
  634.2 254.5 %all-reduce.3.cloned.1.call-done = (f32[256,256]{1,0:T(8,128)}, f32[256,128]{1,0:T(8,128)}) async-done(((f32[256,256]{1,0:T(8,128)}, f32[256,128]{1,0:T(8,128)}), (f32[256,256]{1,0:T(8,128)}, f32[256,128]{1,0:T(8,128)})) %all-reduce.3.cloned.1.call-update) | async-done | bytes 393232 | tf_op jit(solution)/shard_map/psum | solution.py:100
  (113 shorter events, 83.8 us)
Async XLA Ops:
  7.2 226.8 %copy-start = (bf16[256,256]{1,0:T(8,128)(2,1)S(1)}, bf16[256,256]{1,0:T(8,128)(2,1)}, u32[]{:S(2)}) copy-start(bf16[256,256]{1,0:T(8,128)(2,1)} %param.19) | copy-start | bytes 393220
  7.2 89.2 %all-gather.4.cloned.1.call-start = ((), (), s32[]{:S(2)}) async-start(), calls=%async_computation.3 | async-start | bytes 2228224 | tf_op jit(solution)/shard_map/all_gather | solution.py:55
  7.9 226.1 %reduce-scatter.4.cloned.1.call-start = ((), (), s32[]{:S(2)}) async-start(), calls=%async_computation.4 | async-start | bytes 4456448 | tf_op jit(solution)/shard_map/reduce_scatter | solution.py:65
  167.7 105.5 %all-gather.8.cloned.1.call-start = ((), (), s32[]{:S(2)}) async-start(), calls=%async_computation.7 | async-start | bytes 1114112 | tf_op jit(solution)/shard_map/all_gather | solution.py:82
  168.4 189.4 %all-gather.6.cloned.1.call-start = ((), (), s32[]{:S(2)}) async-start(), calls=%async_computation.5 | async-start | bytes 2228224 | tf_op jit(solution)/shard_map/all_gather | solution.py:69
  235.9 324.9 %reduce-scatter.8.cloned.1.call-start = ((), (), s32[]{:S(2)}) async-start(), calls=%async_computation.8 | async-start | bytes 2228224 | tf_op jit(solution)/shard_map/reduce_scatter | solution.py:92
  313.0 319.3 %reduce-scatter.6.cloned.1.call-start = ((), (), s32[]{:S(2)}) async-start(), calls=%async_computation.6 | async-start | bytes 4456448 | tf_op jit(solution)/shard_map/reduce_scatter | solution.py:79
  429.4 131.4 %copy-start.1 = (bf16[256,256]{1,0:T(8,128)(2,1)S(1)}, bf16[256,256]{1,0:T(8,128)(2,1)}, u32[]{:S(2)}) copy-start(bf16[256,256]{1,0:T(8,128)(2,1)} %get-tuple-element.261) | copy-start | bytes 393220
  429.4 133.3 %copy-start.3 = (bf16[256,128]{1,0:T(8,128)(2,1)S(1)}, bf16[256,128]{1,0:T(8,128)(2,1)}, u32[]{:S(2)}) copy-start(bf16[256,128]{1,0:T(8,128)(2,1)} %param.20) | copy-start | bytes 196612
  429.4 134.5 %copy-start.2 = (f32[256,256]{1,0:T(8,128)S(1)}, f32[256,256]{1,0:T(8,128)}, u32[]{:S(2)}) copy-start(f32[256,256]{1,0:T(8,128)} %reduce-scatter.4.cloned.1.call-done) | copy-start | bytes 786436
  429.4 459.3 %all-reduce.3.cloned.1.call-start = ((), (), s32[]{:S(2)}) async-start(), calls=%async_computation.9 | async-start | bytes 786432 | tf_op jit(solution)/shard_map/psum | solution.py:100
Sparse Core Ops, SparseCore 0:
  10.6 85.6 all-gather.3
  167.8 66.1 reduce-scatter.3
  235.9 37.2 all-gather.7
  276.2 81.5 all-gather.5
  361.5 199.2 reduce-scatter.7
  563.2 69.0 reduce-scatter.5
  638.4 250.2 all-reduce.2
where the time goes:
time: 900 us; the launch traced here: 899 us
  waiting for transfers between devices  688 us (76%)
  matrix products  147 us (16%)
  local copies, waits for them, and re-layouts  47.9 us (5%)
  between operations  14.8 us (2%)
    psum x1, waiting for transfers between devices, on_device(): first_grad = lax.psum(first_local, ('row', 'col'))  255 us
    reduce_scatter x1, waiting for transfers between devices, on_device(): lax.psum_scatter(grad_part, 'col', scatter_dimension=0, tiled=True)  131 us
    dot_general x12, matrix products, add_group(): jnp.einsum('tr,taw->raw', select, products, precision=HIGHEST)  99.3 us
    all_gather x1, waiting for transfers between devices, on_device(): gathered_x = lax.all_gather(node_features, 'col', axis=0, tiled=True)  86.8 us
    reduce_scatter x1, waiting for transfers between devices, on_device(): lax.psum_scatter(hidden_part, 'row', scatter_dimension=0, tiled=True)  67.1 us
    reduce_scatter x1, waiting for transfers between devices, on_device(): lax.psum_scatter(feature_part, 'row', scatter_dimension=0, tiled=True)  65.5 us
    all_gather x1, waiting for transfers between devices, on_device(): gathered_h = lax.all_gather(hidden_act, 'col', axis=0, tiled=True)  44.8 us
    dot_general x12, matrix products, add_group(): jnp.einsum(einsum_form, group_tiles, picked, preferred_element_type=jnp.f...  39.1 us
  transfers between devices with their start and end apart: 7, of which 7 were waited for; matrix products, arithmetic and copies ran while one was open for 13% of the time, Pallas kernels for 0%

commit v1 on v0

--- a/solution.py
+++ b/solution.py
@@ -66,7 +66,9 @@
     first_pre = jnp.dot(first_mean, first_weight.astype(jnp.float32), precision=HIGHEST)
     hidden_act = jax.nn.silu(first_pre).astype(jnp.bfloat16)
     second_wide = second_weight.astype(jnp.float32)
-    gathered_h = lax.all_gather(hidden_act, "col", axis=0, tiled=True)
+    gathered_h = jnp.concatenate(
+        lax.all_to_all(jnp.stack([hidden_act] * lax.axis_size("col")), "col", 0, 0), axis=0
+    )
     hidden_part = tile_sum(
         tile_block,
         tile_row,

time: 900 us -> 863 us (0.959)
  waiting for transfers between devices: 688 us -> 641 us
    all_gather x1 -> x0, waiting for transfers between devices: 44.8 us -> none  [on_device(): gathered_h = lax.all_gather(hidden_act, 'col', axis=0, tiled=True)]
  transfers between devices with their start and end apart: 7 -> 7, of which waited for: 7 -> 6; matrix products, arithmetic and copies ran while one was open for 13% -> 14% of each run, Pallas kernels for 0% -> 0%
where the time goes in v1:
time: 863 us; the launch traced here: 861 us
  waiting for transfers between devices  641 us (74%)
  matrix products  146 us (17%)
  local copies, waits for them, and re-layouts  49.3 us (6%)
  between operations  14.8 us (2%)
  starting transfers between devices  9.27 us (1%)
    psum x1, waiting for transfers between devices, on_device(): first_grad = lax.psum(first_local, ('row', 'col'))  254 us
    reduce_scatter x1, waiting for transfers between devices, on_device(): lax.psum_scatter(grad_part, 'col', scatter_dimension=0, tiled=True)  136 us
    dot_general x12, matrix products, add_group(): jnp.einsum('tr,taw->raw', select, products, precision=HIGHEST)  99.1 us
    all_gather x1, waiting for transfers between devices, on_device(): gathered_x = lax.all_gather(node_features, 'col', axis=0, tiled=True)  86.8 us
    reduce_scatter x1, waiting for transfers between devices, on_device(): lax.psum_scatter(hidden_part, 'row', scatter_dimension=0, tiled=True)  66.8 us
    reduce_scatter x1, waiting for transfers between devices, on_device(): lax.psum_scatter(feature_part, 'row', scatter_dimension=0, tiled=True)  65.6 us
    dot_general x12, matrix products, add_group(): jnp.einsum(einsum_form, group_tiles, picked, preferred_element_type=jnp.f...  39 us
    all_gather x1, waiting for transfers between devices, on_device(): gathered_g = lax.all_gather(out_grad, 'row', axis=0, tiled=True)  30.5 us
  transfers between devices with their start and end apart: 7, of which 6 were waited for; matrix products, arithmetic and copies ran while one was open for 14% of the time, Pallas kernels for 0%

profile of v1, /device:TPU:1, one launch (start us, length us, event | category | flops | bytes accessed | tf_op | source)
XLA Modules:
  0.0 861.3 jit_solution(7428008760741438091)
XLA Ops:
  9.6 86.8 %all-gather.3.cloned.1.call-done = bf16[4096,256]{1,0:T(8,128)(2,1)} async-done(((bf16[256,256]{1,0:T(8,128)(2,1)}), bf16[4096,256]{1,0:T(8,128)(2,1)}) %all-gather.3.cloned.1.call-update) | async-done | bytes 2097168 | tf_op jit(solution)/shard_map/all_gather | solution.py:55
  96.3 64.6 %while.33 = (s32[]{:T(128)}, f32[32,128,256]{2,0,1:T(8,128)}, s32[4,32]{1,0:T(4,128)S(1)}, pred[4,32]{1,0:T(4,128)(4,1)S(1)}, bf16[4,32,128,128]{3,2,1,0:T(8,128...) while((s32[]{:T(128)}, f32[32,128,256]{2,0,1:T(8,128)}, ...), condition=%wide.region_1.3_spmd.clone, body=%wide.region_0.2_spmd.clone.sunk | while | flops 674237632 | bytes 24123028 | solution.py:34
  102.6 8.9 %select_add_fusion.6 = f32[32,128,256]{2,0,1:T(8,128)} fusion(f32[32,128,256]{2,0,1:T(8,128)} %get-tuple-element.410, f32[32,128,256]{2,1,0:T(8,128)} %fusion.96, pred[]{:T(512)S(6)} %compare.9, s32[32]{0:T(128)S(1)} %fusion.97, pred[32]{0:T(512)(128)(4,1)S(1)} %dynamic-slice_bitcast_fusion.6), kind=kOutput, calls=%fused_computation.33.clone.1 | convolution fusion | flops 404752384 | bytes 12583073 | tf_op jit(solution)/shard_map/while/body/eval_jaxpr/tr,taw->raw/dot_general | solution.py:30
  117.8 10.2 %select_add_fusion.6 = f32[32,128,256]{2,0,1:T(8,128)} fusion(f32[32,128,256]{2,0,1:T(8,128)} %get-tuple-element.410, f32[32,128,256]{2,1,0:T(8,128)} %fusion.96, pred[]{:T(512)S(6)} %compare.9, s32[32]{0:T(128)S(1)} %fusion.97, pred[32]{0:T(512)(128)(4,1)S(1)} %dynamic-slice_bitcast_fusion.6), kind=kOutput, calls=%fused_computation.33.clone.1 | convolution fusion | flops 404752384 | bytes 12583073 | tf_op jit(solution)/shard_map/while/body/eval_jaxpr/tr,taw->raw/dot_general | solution.py:30
  134.3 10.2 %select_add_fusion.6 = f32[32,128,256]{2,0,1:T(8,128)} fusion(f32[32,128,256]{2,0,1:T(8,128)} %get-tuple-element.410, f32[32,128,256]{2,1,0:T(8,128)} %fusion.96, pred[]{:T(512)S(6)} %compare.9, s32[32]{0:T(128)S(1)} %fusion.97, pred[32]{0:T(512)(128)(4,1)S(1)} %dynamic-slice_bitcast_fusion.6), kind=kOutput, calls=%fused_computation.33.clone.1 | convolution fusion | flops 404752384 | bytes 12583073 | tf_op jit(solution)/shard_map/while/body/eval_jaxpr/tr,taw->raw/dot_general | solution.py:30
  150.7 10.2 %select_add_fusion.6 = f32[32,128,256]{2,0,1:T(8,128)} fusion(f32[32,128,256]{2,0,1:T(8,128)} %get-tuple-element.410, f32[32,128,256]{2,1,0:T(8,128)} %fusion.96, pred[]{:T(512)S(6)} %compare.9, s32[32]{0:T(128)S(1)} %fusion.97, pred[32]{0:T(512)(128)(4,1)S(1)} %dynamic-slice_bitcast_fusion.6), kind=kOutput, calls=%fused_computation.33.clone.1 | convolution fusion | flops 404752384 | bytes 12583073 | tf_op jit(solution)/shard_map/while/body/eval_jaxpr/tr,taw->raw/dot_general | solution.py:30
  160.9 6.6 copy.10
  168.3 65.6 %reduce-scatter.4.cloned.1.call-done = f32[256,256]{1,0:T(8,128)} async-done(((f32[4096,256]{1,0:T(8,128)}), f32[256,256]{1,0:T(8,128)}) %reduce-scatter.4.cloned.1.call-update) | async-done | bytes 262160 | tf_op jit(solution)/shard_map/reduce_scatter | solution.py:65
  237.3 8.9 %all-to-all-start = ((bf16[16,256,256]{2,1,0:T(8,128)(2,1)}), bf16[16,256,256]{2,1,0:T(8,128)(2,1)}, u32[]{:S(2)}, u32[]{:S(2)}) async-start(bf16[16,256,256]{2,1,0:T(8,128)(2,1)} %stack.2), calls=%async_computation.1 | async-start | bytes 4194304 | tf_op jit(solution)/shard_map/all_to_all | solution.py:70
  246.4 30.5 %all-gather.5.cloned.1.call-done = bf16[4096,128]{1,0:T(8,128)(2,1)} async-done(((bf16[256,128]{1,0:T(8,128)(2,1)}), bf16[4096,128]{1,0:T(8,128)(2,1)}) %all-gather.5.cloned.1.call-update) | async-done | bytes 1048592 | tf_op jit(solution)/shard_map/all_gather | solution.py:84
  276.9 35.6 %while.35 = (s32[]{:T(128)}, f32[32,128,128]{2,0,1:T(8,128)}, s32[4,32]{1,0:T(4,128)S(1)}, pred[4,32]{1,0:T(4,128)(4,1)S(1)}, bf16[4,32,128,128]{3,2,1,0:T(8,128...) while((s32[]{:T(128)}, f32[32,128,128]{2,0,1:T(8,128)}, ...), condition=%wide.region_7.9_spmd.clone, body=%wide.region_6.8_spmd.clone.sunk | while | flops 337120544 | bytes 12588823 | solution.py:34
  288.4 5.4 select_add_fusion.8
  297.7 5.4 select_add_fusion.8
  307.0 5.4 select_add_fusion.8
  312.5 4.1 copy.12
  316.7 64.8 %while.34 = (s32[]{:T(128)}, f32[32,128,256]{2,0,1:T(8,128)}, s32[4,32]{1,0:T(4,128)S(1)}, pred[4,32]{1,0:T(4,128)(4,1)S(1)}, bf16[4,32,128,128]{3,2,1,0:T(8,128...) while((s32[]{:T(128)}, f32[32,128,256]{2,0,1:T(8,128)}, ...), condition=%wide.region_4.6_spmd.clone, body=%wide.region_3.5_spmd.clone.sunk | while | flops 674237632 | bytes 24123028 | solution.py:34
  323.0 8.9 %select_add_fusion.7 = f32[32,128,256]{2,0,1:T(8,128)} fusion(f32[32,128,256]{2,0,1:T(8,128)} %get-tuple-element.437, f32[32,128,256]{2,1,0:T(8,128)} %fusion.102, pred[]{:T(512)S(6)} %compare.10, s32[32]{0:T(128)S(1)} %fusion.103, pred[32]{0:T(512)(128)(4,1)S(1)} %dynamic-slice_bitcast_fusion.7), kind=kOutput, calls=%fused_computation.57.clone.1 | convolution fusion | flops 404752384 | bytes 12583073 | tf_op jit(solution)/shard_map/while/body/eval_jaxpr/tr,taw->raw/dot_general | solution.py:30
  338.2 10.2 %select_add_fusion.7 = f32[32,128,256]{2,0,1:T(8,128)} fusion(f32[32,128,256]{2,0,1:T(8,128)} %get-tuple-element.437, f32[32,128,256]{2,1,0:T(8,128)} %fusion.102, pred[]{:T(512)S(6)} %compare.10, s32[32]{0:T(128)S(1)} %fusion.103, pred[32]{0:T(512)(128)(4,1)S(1)} %dynamic-slice_bitcast_fusion.7), kind=kOutput, calls=%fused_computation.57.clone.1 | convolution fusion | flops 404752384 | bytes 12583073 | tf_op jit(solution)/shard_map/while/body/eval_jaxpr/tr,taw->raw/dot_general | solution.py:30
  354.7 10.2 %select_add_fusion.7 = f32[32,128,256]{2,0,1:T(8,128)} fusion(f32[32,128,256]{2,0,1:T(8,128)} %get-tuple-element.437, f32[32,128,256]{2,1,0:T(8,128)} %fusion.102, pred[]{:T(512)S(6)} %compare.10, s32[32]{0:T(128)S(1)} %fusion.103, pred[32]{0:T(512)(128)(4,1)S(1)} %dynamic-slice_bitcast_fusion.7), kind=kOutput, calls=%fused_computation.57.clone.1 | convolution fusion | flops 404752384 | bytes 12583073 | tf_op jit(solution)/shard_map/while/body/eval_jaxpr/tr,taw->raw/dot_general | solution.py:30
  371.2 10.2 %select_add_fusion.7 = f32[32,128,256]{2,0,1:T(8,128)} fusion(f32[32,128,256]{2,0,1:T(8,128)} %get-tuple-element.437, f32[32,128,256]{2,1,0:T(8,128)} %fusion.102, pred[]{:T(512)S(6)} %compare.10, s32[32]{0:T(128)S(1)} %fusion.103, pred[32]{0:T(512)(128)(4,1)S(1)} %dynamic-slice_bitcast_fusion.7), kind=kOutput, calls=%fused_computation.57.clone.1 | convolution fusion | flops 404752384 | bytes 12583073 | tf_op jit(solution)/shard_map/while/body/eval_jaxpr/tr,taw->raw/dot_general | solution.py:30
  381.4 6.6 copy.11
  388.1 135.8 %reduce-scatter.8.cloned.1.call-done = f32[256,128]{1,0:T(8,128)} async-done(((f32[4096,128]{1,0:T(8,128)}), f32[256,128]{1,0:T(8,128)}) %reduce-scatter.8.cloned.1.call-update) | async-done | bytes 131088 | tf_op jit(solution)/shard_map/reduce_scatter | solution.py:94
  528.3 66.8 %reduce-scatter.6.cloned.1.call-done = f32[256,256]{1,0:T(8,128)} async-done(((f32[4096,256]{1,0:T(8,128)}), f32[256,256]{1,0:T(8,128)}) %reduce-scatter.6.cloned.1.call-update) | async-done | bytes 262160 | tf_op jit(solution)/shard_map/reduce_scatter | solution.py:81
  596.9 254.4 %all-reduce.3.cloned.1.call-done = (f32[256,256]{1,0:T(8,128)}, f32[256,128]{1,0:T(8,128)}) async-done(((f32[256,256]{1,0:T(8,128)}, f32[256,128]{1,0:T(8,128)}), (f32[256,256]{1,0:T(8,128)}, f32[256,128]{1,0:T(8,128)})) %all-reduce.3.cloned.1.call-update) | async-done | bytes 393232 | tf_op jit(solution)/shard_map/psum | solution.py:102
  (113 shorter events, 85.1 us)
Async XLA Ops:
  7.2 226.7 %copy-start = (bf16[256,256]{1,0:T(8,128)(2,1)S(1)}, bf16[256,256]{1,0:T(8,128)(2,1)}, u32[]{:S(2)}) copy-start(bf16[256,256]{1,0:T(8,128)(2,1)} %param.19) | copy-start | bytes 393220
  7.2 89.2 %all-gather.3.cloned.1.call-start = ((), (), s32[]{:S(2)}) async-start(), calls=%async_computation.4 | async-start | bytes 2228224 | tf_op jit(solution)/shard_map/all_gather | solution.py:55
  7.9 225.9 %reduce-scatter.4.cloned.1.call-start = ((), (), s32[]{:S(2)}) async-start(), calls=%async_computation.5 | async-start | bytes 4456448 | tf_op jit(solution)/shard_map/reduce_scatter | solution.py:65
  167.5 109.3 %all-gather.5.cloned.1.call-start = ((), (), s32[]{:S(2)}) async-start(), calls=%async_computation.7 | async-start | bytes 1114112 | tf_op jit(solution)/shard_map/all_gather | solution.py:84
  237.3 79.4 %all-to-all-start = ((bf16[16,256,256]{2,1,0:T(8,128)(2,1)}), bf16[16,256,256]{2,1,0:T(8,128)(2,1)}, u32[]{:S(2)}, u32[]{:S(2)}) async-start(bf16[16,256,256]{2,1,0:T(8,128)(2,1)} %stack.2), calls=%async_computation.1 | async-start | bytes 4194304 | tf_op jit(solution)/shard_map/all_to_all | solution.py:70
  246.2 277.7 %reduce-scatter.8.cloned.1.call-start = ((), (), s32[]{:S(2)}) async-start(), calls=%async_computation.8 | async-start | bytes 2228224 | tf_op jit(solution)/shard_map/reduce_scatter | solution.py:94
  316.6 278.4 %reduce-scatter.6.cloned.1.call-start = ((), (), s32[]{:S(2)}) async-start(), calls=%async_computation.6 | async-start | bytes 4456448 | tf_op jit(solution)/shard_map/reduce_scatter | solution.py:81
  388.0 137.7 %copy-start.2 = (bf16[256,128]{1,0:T(8,128)(2,1)S(1)}, bf16[256,128]{1,0:T(8,128)(2,1)}, u32[]{:S(2)}) copy-start(bf16[256,128]{1,0:T(8,128)(2,1)} %param.20) | copy-start | bytes 196612
  388.0 137.7 %copy-start.3 = (f32[256,256]{1,0:T(8,128)S(1)}, f32[256,256]{1,0:T(8,128)}, u32[]{:S(2)}) copy-start(f32[256,256]{1,0:T(8,128)} %get-tuple-element.262) | copy-start | bytes 786436
  388.0 138.9 %copy-start.1 = (f32[256,256]{1,0:T(8,128)S(1)}, f32[256,256]{1,0:T(8,128)}, u32[]{:S(2)}) copy-start(f32[256,256]{1,0:T(8,128)} %reduce-scatter.4.cloned.1.call-done) | copy-start | bytes 786436
  388.1 463.2 %all-reduce.3.cloned.1.call-start = ((), (), s32[]{:S(2)}) async-start(), calls=%async_computation.9 | async-start | bytes 786432 | tf_op jit(solution)/shard_map/psum | solution.py:102
Sparse Core Ops, SparseCore 0:
  10.6 85.6 all-gather.2
  167.6 66.1 reduce-scatter.3
  235.7 41.1 all-gather.4
  316.7 207.0 reduce-scatter.7
  526.3 68.7 reduce-scatter.5
  601.0 250.1 all-reduce.2
